TPU v7x, 32 devices: a whole 2x2x4 slice. The times are simulated.
32 devices in a mesh: ka: 16 (over z, x, core), ga: 2 (over y).
Axes of the slice: x: 2, y: 2, z: 4, core: 2. Of those that a mesh axis runs over, the one named last changes fastest.
Arguments:
- pair_density: bfloat16 [128, 32, 12032], P('ka', None, 'ga'), may hold values from -6 to 6
- coulomb: float32 [12032], P('ga'), may hold values from 3e-05 to 0.003
Outputs:
- kernel: float32 [4096, 1280], P(('ka', 'ga'))
All inputs are finite; a program needn't handle non-finite values.
Results may differ from a plain program's by a relative error of at most 0.0013.
Values may be sent and summed in bfloat16 or wider, within the bound.
A program may use at most 64 MiB of HBM per device.

v0:
```python
import jax
import jax.numpy as jnp
from jax import lax
from jax.sharding import PartitionSpec as P

STEPS = 2


def shifted(value, axis, steps):
    count = lax.axis_size(axis)
    pairs = [(source, (source + steps) % count) for source in range(count)]
    return lax.ppermute(value, axis, pairs)


def product(left, right):
    return lax.dot_general(
        left, right, (((1,), (1,)), ((), ())), preferred_element_type=jnp.float32
    )


def shards(pair_density, coulomb):
    shard_points, pairs, local_waves = pair_density.shape
    width = shard_points * pairs
    own = pair_density.reshape(width, local_waves)
    weighted = (own.astype(jnp.float32) * coulomb[None, :]).astype(jnp.bfloat16)
    lower_blocks = [None] * (STEPS + 1)
    upper_blocks = [None] * (STEPS + 1)
    lower_blocks[0] = product(weighted, own)
    current = pair_density
    for step in range(1, STEPS + 1):
        current = shifted(current, "ka", 1)
        block = product(weighted, current.reshape(width, local_waves))
        lower_blocks[step] = block
        upper_blocks[step] = shifted(block.T, "ka", -step)
    ordered = [lower_blocks[step] for step in range(STEPS, -1, -1)]
    joined_blocks = ordered + [upper_blocks[step] for step in range(1, STEPS + 1)]
    stacked = jnp.concatenate(joined_blocks, axis=1)
    summed = lax.psum_scatter(stacked, "ga", scatter_dimension=0, tiled=True)
    return summed


def solution(mesh):
    in_specs = (P("ka", None, "ga"), P("ga"))
    out_specs = P(("ka", "ga"), None)
    return jax.shard_map(shards, mesh=mesh, in_specs=in_specs, out_specs=out_specs, check_vma=False)
```

profile of v0, /device:TPU:0, one launch (start us, length us, event | category | flops | bytes accessed | tf_op | source)
XLA Modules:
  0.0 135.7 jit_solution(9870011628428674851)
XLA Ops:
  6.5 0.0 reduce-scatter.2.cloned.1.call-start
  6.5 0.5 collective-permute-start
  7.0 39.4 %collective-permute-done = bf16[8,32,6016]{2,1,0:T(8,128)(2,1)S(1)} collective-permute-done((bf16[8,32,6016]{2,1,0:T(8,128)(2,1)}, bf16[8,32,6016]{2,1,0:T(8,128)(2,1)S(1)}, u32[]{:S(2)}, u32[]{:S(2)}) %collective-permute-start) | collective-permute-done | bytes 3080224 | tf_op jit(solution)/shard_map/ppermute | solution.py:12
  46.4 0.0 collective-permute-start.1
  46.4 2.4 %multiply_convert_fusion = bf16[8,32,6016]{2,1,0:T(8,128)(2,1)S(1)} fusion(bf16[8,32,6016]{2,1,0:T(8,128)(2,1)} %param.2, f32[6016]{0:T(1024)} %param.3), kind=kLoop, calls=%fused_computation | loop fusion | flops 4620288 | bytes 6184448 | tf_op jit(solution)/shard_map/convert_element_type | solution.py:25
  48.8 36.3 %collective-permute-done.1 = bf16[8,32,6016]{2,1,0:T(8,128)(2,1)S(1)} collective-permute-done((bf16[8,32,6016]{2,1,0:T(8,128)(2,1)S(1)}, bf16[8,32,6016]{2,1,0:T(8,128)(2,1)S(1)}, u32[]{:S(2)}, u32[]{:S(2)}) %collective-permute-start.1) | collective-permute-done | bytes 3080224 | tf_op jit(solution)/shard_map/ppermute | solution.py:12
  85.1 1.0 constant_dynamic-update-slice_fusion.3
  86.1 1.7 %constant_dynamic-update-slice_fusion.2 = (f32[256,1280]{0,1:T(8,128)S(1)}, f32[256,256]{0,1:T(8,128)}) fusion(f32[256,1280]{0,1:T(8,128)S(1)} %get-tuple-element.5, bf16[256,6016]{1,0:T(8,128)(2,1)S(1)} %bitcast.13, bf16[256,6016]{1,0:T(8,128)(2,1)S(1)} %bitcast.16), kind=kOutput, calls=%fused_computation.4 | convolution fusion | flops 788529152 | bytes 6684672 | tf_op jit(solution)/shard_map/dot_general | solution.py:16
  87.9 0.0 copy-start
  87.9 1.1 copy-done
  88.9 1.8 %copy.3 = f32[256,256]{1,0:T(8,128)} copy(f32[256,256]{0,1:T(8,128)} %get-tuple-element.8) | data formatting | bytes 524288 | tf_op jit(solution)/shard_map/dot_general | solution.py:16
  90.7 0.8 copy.4
  91.5 0.0 collective-permute-start.3
  91.5 0.0 collective-permute-start.2
  91.5 3.6 %convolution_dynamic-update-slice_fusion = f32[256,1280]{0,1:T(8,128)} fusion(f32[256,1280]{0,1:T(8,128)} %copy-done, bf16[256,6016]{1,0:T(8,128)(2,1)S(1)} %bitcast.14, bf16[256,6016]{1,0:T(8,128)(2,1)} %bitcast.15), kind=kOutput, calls=%fused_computation.1 | convolution fusion | flops 788529152 | bytes 6422528 | tf_op jit(solution)/shard_map/dot_general | solution.py:16
  95.1 4.9 %collective-permute-done.2 = f32[256,256]{0,1:T(8,128)S(1)} collective-permute-done((f32[256,256]{0,1:T(8,128)}, f32[256,256]{0,1:T(8,128)S(1)}, u32[]{:S(2)}, u32[]{:S(2)}) %collective-permute-start.2) | collective-permute-done | bytes 262176 | tf_op jit(solution)/shard_map/ppermute | solution.py:12
  100.1 0.7 constant_dynamic-update-slice_fusion.1
  100.8 0.0 collective-permute-done.3
  100.8 0.7 constant_dynamic-update-slice_fusion
  101.5 0.0 reduce-scatter.2.cloned.1.call-update
  101.5 25.2 %reduce-scatter.2.cloned.1.call-done = f32[128,1280]{0,1:T(8,128)} async-done(((f32[256,1280]{0,1:T(8,128)}), f32[128,1280]{0,1:T(8,128)}) %reduce-scatter.2.cloned.1.call-update) | async-done | bytes 655376 | tf_op jit(solution)/shard_map/reduce_scatter | solution.py:38
  126.7 2.2 %copy.5 = f32[128,1280]{1,0:T(8,128)} copy(f32[128,1280]{0,1:T(8,128)} %reduce-scatter.2.cloned.1.call-done) | data formatting | bytes 1310720 | tf_op jit(solution)/shard_map/reduce_scatter | solution.py:38
Async XLA Ops:
  6.5 120.1 %reduce-scatter.2.cloned.1.call-start = ((), (), s32[]{:S(2)}) async-start(), calls=%async_computation.1 | async-start | bytes 1966080 | tf_op jit(solution)/shard_map/reduce_scatter | solution.py:38
  6.5 39.9 %collective-permute-start = (bf16[8,32,6016]{2,1,0:T(8,128)(2,1)}, bf16[8,32,6016]{2,1,0:T(8,128)(2,1)S(1)}, u32[]{:S(2)}, u32[]{:S(2)}) collective-permute-start(bf16[8,32,6016]{2,1,0:T(8,128)(2,1)} %param.2), channel_id=1, source_target_pairs={{0,2},{2,4},{4,6},{6,8},{8,10},{10,12},{12,14},{14,16},{16,18},{18... | collective-permute-start | bytes 9240584 | tf_op jit(solution)/shard_map/ppermute | solution.py:12
  46.4 38.7 %collective-permute-start.1 = (bf16[8,32,6016]{2,1,0:T(8,128)(2,1)S(1)}, bf16[8,32,6016]{2,1,0:T(8,128)(2,1)S(1)}, u32[]{:S(2)}, u32[]{:S(2)}) collective-permute-start(bf16[8,32,6016]{2,1,0:T(8,128)(2,1)S(1)} %collective-permute-done), channel_id=1, source_target_pairs={{0,2},{2,4},{4,6},{6,8},{8,10},{10,12},{12,14},{14,16},{16,18},{18... | collective-permute-start | bytes 9240584 | tf_op jit(solution)/shard_map/ppermute | solution.py:12
  87.9 1.1 copy-start
  91.5 9.2 %collective-permute-start.3 = (f32[256,256]{0,1:T(8,128)}, f32[256,256]{0,1:T(8,128)S(1)}, u32[]{:S(2)}, u32[]{:S(2)}) collective-permute-start(f32[256,256]{0,1:T(8,128)} %bitcast.18), channel_id=1, source_target_pairs={{0,28},{2,30},{4,0},{6,2},{8,4},{10,6},{12,8},{14,10},{16,12},{18,... | collective-permute-start | bytes 786440 | tf_op jit(solution)/shard_map/ppermute | solution.py:12
  91.5 8.5 %collective-permute-start.2 = (f32[256,256]{0,1:T(8,128)}, f32[256,256]{0,1:T(8,128)S(1)}, u32[]{:S(2)}, u32[]{:S(2)}) collective-permute-start(f32[256,256]{0,1:T(8,128)} %bitcast.19), channel_id=1, source_target_pairs={{0,30},{2,0},{4,2},{6,4},{8,6},{10,8},{12,10},{14,12},{16,14},{18,... | collective-permute-start | bytes 786440 | tf_op jit(solution)/shard_map/ppermute | solution.py:12
Sparse Core Ops, SparseCore 0:
  101.6 24.9 reduce-scatter.1
where the time goes:
time: 136 us
  waiting for transfers between devices  106 us (78%)
  between operations  13.4 us (10%)
  local copies, waits for them, and re-layouts  7.27 us (5%)
  matrix products  6.29 us (5%)
  other arithmetic  2.37 us (2%)
    ppermute x4, waiting for transfers between devices, shifted(): return lax.ppermute(value, axis, pairs)  80.7 us
    reduce_scatter x1, waiting for transfers between devices, shards(): summed = lax.psum_scatter(stacked, 'ga', scatter_dimension=0, tiled=True)  25.2 us
    dot_general x3, matrix products, product(): lax.dot_general(left, right, (((1,), (1,)), ((), ())), preferred_element_...  6.29 us
  transfers between devices with their start and end apart: 5, of which 4 were waited for; matrix products, arithmetic and copies ran while one was open for 5% of the time, Pallas kernels for 0%

commit v1 on v0

v1 whole, which is shorter than its diff:
```python
import functools

import jax
import jax.numpy as jnp
from jax import lax
from jax.experimental import pallas as pl
from jax.experimental.pallas import tpu as pltpu
from jax.sharding import PartitionSpec as P

LANES = 128
GROUP = 4
MESH = pl.DeviceIdType.MESH


def product(left, right):
    return lax.dot_general(
        left, right, (((1,), (1,)), ((), ())), preferred_element_type=jnp.float32
    )


def weigh(rows, scale):
    return (rows.astype(jnp.float32) * scale).astype(jnp.bfloat16)


def plan(tiles):
    piece = -(-tiles // GROUP)
    depth = 2 if piece % 2 == 0 else 1
    return piece, depth, piece // depth


def kernel(
    count, own_hbm, coulomb_ref, out_ref,
    own_ref, slab, sums, diag, got_core, got_half, half, got_x, got_diag, turned, got_turned,
    own_sem, local_sem, a2a_send, a2a_recv, fwd_send, fwd_recv,
    red_send, red_recv, turn_send, turn_recv,
):
    me = lax.axis_index("ka")
    side = lax.axis_index("ga")
    width, waves = own_ref.shape
    rows = width // 2
    tiles = waves // LANES
    piece, depth, chunks = plan(tiles)
    span = depth * LANES
    rank = lax.rem(me, GROUP)
    base = me - rank
    core = lax.rem(rank, 2)
    column = rank // 2
    up = lax.rem(me + GROUP, count)
    down = lax.rem(me + count - GROUP, count)
    partners = (
        2 * (1 - column) + core,
        2 * (1 - column) + 1 - core,
        2 * column + 1 - core,
    )

    def at(ka, ga):
        return {"ka": ka, "ga": ga}

    barrier = pltpu.get_barrier_semaphore()
    greeted = [at(base + p, side) for p in partners]
    greeted += [at(up, side), at(down, side), at(me, 1 - side)]
    for shift in (1, 2):
        for other in (0, 1):
            greeted.append(at(lax.rem(me + shift, count), other))
            greeted.append(at(lax.rem(me + count - shift, count), other))
    for target in greeted:
        pl.semaphore_signal(barrier, inc=1, device_id=target, device_id_type=MESH)

    def first_wave(r):
        return jnp.minimum(r * piece, tiles - piece) * LANES

    def remote(src, dst, send, recv, target):
        return pltpu.make_async_remote_copy(
            src_ref=src, dst_ref=dst, send_sem=send, recv_sem=recv,
            device_id=target, device_id_type=MESH,
        )

    def window(r, chunk):
        return pl.ds(pl.multiple_of(first_wave(r) + chunk * span, LANES), span)

    def spread(chunk, index):
        target = partners[index]
        return remote(
            own_hbm.at[:, window(target, chunk)], slab.at[chunk, 2 + rank],
            a2a_send.at[index, chunk], a2a_recv.at[index, chunk], at(base + target, side),
        )

    def local(chunk):
        return pltpu.make_async_copy(
            own_hbm.at[:, window(rank, chunk)], slab.at[chunk, 2 + rank], local_sem.at[chunk]
        )

    def forward(chunk):
        return remote(
            slab.at[chunk, pl.ds(GROUP, 2)], slab.at[chunk, pl.ds(0, 2)],
            fwd_send.at[chunk], fwd_recv.at[chunk], at(up, side),
        )

    whole = pltpu.make_async_copy(own_hbm, own_ref, own_sem)
    whole.start()
    for chunk in range(chunks):
        local(chunk).start()
    pl.semaphore_wait(barrier, len(greeted))
    for chunk in range(chunks):
        for index in range(3):
            spread(chunk, index).start()

    whole.wait()
    diag[...] = jnp.zeros_like(diag)

    def add_diag(start, size):
        mine = own_ref[:, pl.ds(start, size)]
        diag[...] += product(weigh(mine, coulomb_ref[:, pl.ds(start, size)]), mine)

    @pl.loop(0, tiles // 2)
    def _(step):
        add_diag(pl.multiple_of(step * 2 * LANES, LANES), 2 * LANES)

    if tiles % 2:
        add_diag((tiles - 1) * LANES, LANES)
    my_rows = pl.ds(pl.multiple_of(side * rows, rows), rows)
    their_rows = pl.ds(pl.multiple_of((1 - side) * rows, rows), rows)
    send_diag = remote(
        diag.at[their_rows], got_diag, red_send.at[3], red_recv.at[3], at(me, 1 - side)
    )
    send_diag.start()

    sums[...] = jnp.zeros_like(sums)

    def scale_of(chunk):
        start = first_wave(rank) + chunk * span
        scale = coulomb_ref[:, pl.ds(pl.multiple_of(start, LANES), span)]
        wave = start + lax.broadcasted_iota(jnp.int32, (1, span), 1)
        return jnp.where(wave >= rank * piece * LANES, scale, 0.0)

    def add_block(chunk, scale, shard, steps):
        left = weigh(slab[chunk, 2 + shard], scale)
        for step in steps:
            where = pl.ds((2 - step) * width, width)
            sums[shard % 2, shard // 2, :, where] += product(left, slab[chunk, 2 + shard - step])

    @pl.loop(0, chunks)
    def _(chunk):
        local(chunk).wait()
        for index in range(3):
            spread(chunk, index).wait_recv()
        forward(chunk).start()
        scale = scale_of(chunk)
        add_block(chunk, scale, 1, (1,))
        add_block(chunk, scale, 2, (2, 1))
        add_block(chunk, scale, 3, (2, 1))

    @pl.loop(0, chunks)
    def _(chunk):
        forward(chunk).wait_recv()
        scale = scale_of(chunk)
        add_block(chunk, scale, 0, (2, 1))
        add_block(chunk, scale, 1, (2,))

    to_core = remote(
        sums.at[1 - core], got_core, red_send.at[0], red_recv.at[0], at(base + partners[2], side)
    )
    to_core.start()
    to_core.wait()
    sums[core] += got_core[...]
    to_half = remote(
        sums.at[core, :, their_rows], got_half, red_send.at[1], red_recv.at[1], at(me, 1 - side)
    )
    to_half.start()
    to_half.wait()
    half[...] = sums[core, :, my_rows] + got_half[...]
    to_x = remote(
        half.at[1 - column], got_x, red_send.at[2], red_recv.at[2], at(base + partners[0], side)
    )
    to_x.start()
    to_x.wait()
    lower = half[column] + got_x[...]
    out_ref[:, 0 : 2 * width] = lower

    def turn(step, other):
        slot = (step - 1) * 2 + other
        return remote(
            turned.at[slot], got_turned.at[step - 1, side],
            turn_send.at[slot], turn_recv.at[step - 1, side],
            at(lax.rem(me + count - step, count), other),
        )

    for step in (2, 1):
        for other in (0, 1):
            begin = (2 - step) * width + other * rows
            turned[(step - 1) * 2 + other] = lower[:, begin : begin + rows].T
            turn(step, other).start()
    send_diag.wait()
    out_ref[:, 2 * width : 3 * width] = diag[my_rows, :] + got_diag[...]
    for step in (2, 1):
        for other in (0, 1):
            pltpu.make_async_copy(
                got_turned.at[step - 1, other], got_turned.at[step - 1, other],
                turn_recv.at[step - 1, other],
            ).wait()
            begin = (2 + step) * width + other * rows
            out_ref[:, begin : begin + rows] = got_turned[step - 1, other]
    for step in (2, 1):
        for other in (0, 1):
            turn(step, other).wait_send()

    @pl.loop(0, chunks)
    def _(chunk):
        forward(chunk).wait_send()
        for index in range(3):
            spread(chunk, index).wait_send()


def shards(count, pair_density, coulomb):
    shard_points, pairs, waves = pair_density.shape
    width = shard_points * pairs
    rows = width // 2
    piece, depth, chunks = plan(waves // LANES)
    span = depth * LANES
    wide = 2 * width
    dma = pltpu.SemaphoreType.DMA
    return pl.pallas_call(
        functools.partial(kernel, count),
        out_shape=jax.ShapeDtypeStruct((rows, 5 * width), jnp.float32),
        in_specs=[
            pl.BlockSpec(memory_space=pl.ANY),
            pl.BlockSpec(memory_space=pltpu.VMEM),
        ],
        out_specs=pl.BlockSpec(memory_space=pltpu.VMEM),
        scratch_shapes=[
            pltpu.VMEM((width, waves), jnp.bfloat16),
            pltpu.VMEM((chunks, GROUP + 2, width, span), jnp.bfloat16),
            pltpu.VMEM((2, 2, width, wide), jnp.float32),
            pltpu.VMEM((width, width), jnp.float32),
            pltpu.VMEM((2, width, wide), jnp.float32),
            pltpu.VMEM((2, rows, wide), jnp.float32),
            pltpu.VMEM((2, rows, wide), jnp.float32),
            pltpu.VMEM((rows, wide), jnp.float32),
            pltpu.VMEM((rows, width), jnp.float32),
            pltpu.VMEM((4, rows, rows), jnp.float32),
            pltpu.VMEM((2, 2, rows, rows), jnp.float32),
            dma, dma((chunks,)), dma((3, chunks)), dma((3, chunks)),
            dma((chunks,)), dma((chunks,)), dma((4,)), dma((4,)), dma((4,)), dma((2, 2)),
        ],
        compiler_params=pltpu.CompilerParams(
            collective_id=0, has_side_effects=True, vmem_limit_bytes=48 * 1024 * 1024
        ),
    )(pair_density.reshape(width, waves), coulomb.reshape(1, waves))


def solution(mesh):
    in_specs = (P("ka", None, "ga"), P("ga"))
    out_specs = P(("ka", "ga"), None)
    body = functools.partial(shards, mesh.shape["ka"])
    return jax.shard_map(body, mesh=mesh, in_specs=in_specs, out_specs=out_specs, check_vma=False)
```

time: 136 us -> 81.7 us (0.60)
  waiting for transfers between devices: 106 us -> 0 us
  Pallas kernels: 0 us -> 77.5 us
  between operations: 13.4 us -> 0.02 us
  matrix products: 6.29 us -> 0 us
  local copies, waits for them, and re-layouts: 7.27 us -> 3.46 us
  other arithmetic: 2.37 us -> 0 us
    ppermute x4 -> x0, waiting for transfers between devices: 80.7 us -> none  [shifted(): return lax.ppermute(value, axis, pairs)]
    pallas_call x0 -> x1, Pallas kernels: none -> 77.5 us  [shards(): pl.pallas_call(functools.partial(kernel, count), out_shape=jax.ShapeDtype...]
    reduce_scatter x1 -> x0, waiting for transfers between devices: 25.2 us -> none  [shards(): summed = lax.psum_scatter(stacked, 'ga', scatter_dimension=0, tiled=True)]
    dot_general x3 -> x0, matrix products: 6.29 us -> none  [product(): lax.dot_general(left, right, (((1,), (1,)), ((), ())), preferred_element_...]
    dot_general x2 -> x0, local copies, waits for them, and re-layouts: 2.61 us -> none  [product(): lax.dot_general(left, right, (((1,), (1,)), ((), ())), preferred_element_...]
    convert_element_type x1 -> x0, other arithmetic: 2.37 us -> none  [shards(): weighted = (own.astype(jnp.float32) * coulomb[None, :]).astype(jnp.bfloat16)]
    reduce_scatter x1 -> x0, local copies, waits for them, and re-layouts: 2.16 us -> none  [shards(): summed = lax.psum_scatter(stacked, 'ga', scatter_dimension=0, tiled=True)]
  transfers between devices with their start and end apart: 5 -> 0, of which waited for: 4 -> 0; matrix products, arithmetic and copies ran while one was open for 5% -> 0% of each run, Pallas kernels for 0% -> 0%
where the time goes in v1:
time: 81.7 us; the launch traced here: 81 us
  Pallas kernels  77.5 us (95%)
  local copies, waits for them, and re-layouts  3.46 us (4%)
    pallas_call x1, Pallas kernels, shards(): pl.pallas_call(functools.partial(kernel, count), out_shape=jax.ShapeDtype...  77.5 us
    unnamed x3, local copies, waits for them, and re-layouts  2.7 us

profile of v1, /device:TPU:0, one launch (start us, length us, event | category | flops | bytes accessed | tf_op | source)
XLA Modules:
  0.0 81.0 jit_solution(3004304964092347433)
XLA Ops:
  0.0 0.8 reshape.7.coulomb_ref
  0.8 0.0 copy-start
  0.8 1.9 %copy-done = bf16[8,32,6016]{2,1,0:T(8,128)(2,1)S(1)} copy-done((bf16[8,32,6016]{2,1,0:T(8,128)(2,1)S(1)}, bf16[8,32,6016]{2,1,0:T(8,128)(2,1)}, u32[]{:S(2)}) %copy-start) | copy-done | bytes 3080216
  2.6 77.5 %shard_map.28 = f32[128,1280]{1,0:T(8,128)S(1)} custom-call(bf16[256,6016]{1,0:T(8,128)(2,1)S(1)} %bitcast.1, f32[1,6016]{1,0:T(1,128)S(1)} %reshape.7.coulomb_ref), custom_call_target="tpu_custom_call" | custom-call | tf_op jit(solution)/shard_map/pallas_call | solution.py:222
  80.1 0.8 %copy.4 = f32[128,1280]{1,0:T(8,128)} copy(f32[128,1280]{1,0:T(8,128)S(1)} %shard_map.28) | data formatting | bytes 1310720
Async XLA Ops:
  0.8 1.9 %copy-start = (bf16[8,32,6016]{2,1,0:T(8,128)(2,1)S(1)}, bf16[8,32,6016]{2,1,0:T(8,128)(2,1)}, u32[]{:S(2)}) copy-start(bf16[8,32,6016]{2,1,0:T(8,128)(2,1)} %param.2) | copy-start | bytes 9240580

commit v2 on v1

--- a/solution.py
+++ b/solution.py
@@ -121,7 +121,7 @@
     my_rows = pl.ds(pl.multiple_of(side * rows, rows), rows)
     their_rows = pl.ds(pl.multiple_of((1 - side) * rows, rows), rows)
     send_diag = remote(
-        diag.at[their_rows], got_diag, red_send.at[3], red_recv.at[3], at(me, 1 - side)
+        diag.at[their_rows], got_diag, red_send.at[10], red_recv.at[10], at(me, 1 - side)
     )
     send_diag.start()
 
@@ -139,8 +139,7 @@
             where = pl.ds((2 - step) * width, width)
             sums[shard % 2, shard // 2, :, where] += product(left, slab[chunk, 2 + shard - step])
 
-    @pl.loop(0, chunks)
-    def _(chunk):
+    def arrive(chunk):
         local(chunk).wait()
         for index in range(3):
             spread(chunk, index).wait_recv()
@@ -150,32 +149,78 @@
         add_block(chunk, scale, 2, (2, 1))
         add_block(chunk, scale, 3, (2, 1))
 
-    @pl.loop(0, chunks)
-    def _(chunk):
+    def arrive_below(chunk):
         forward(chunk).wait_recv()
         scale = scale_of(chunk)
         add_block(chunk, scale, 0, (2, 1))
         add_block(chunk, scale, 1, (2,))
 
-    to_core = remote(
-        sums.at[1 - core], got_core, red_send.at[0], red_recv.at[0], at(base + partners[2], side)
-    )
-    to_core.start()
-    to_core.wait()
-    sums[core] += got_core[...]
-    to_half = remote(
-        sums.at[core, :, their_rows], got_half, red_send.at[1], red_recv.at[1], at(me, 1 - side)
-    )
-    to_half.start()
-    to_half.wait()
-    half[...] = sums[core, :, my_rows] + got_half[...]
-    to_x = remote(
-        half.at[1 - column], got_x, red_send.at[2], red_recv.at[2], at(base + partners[0], side)
-    )
-    to_x.start()
-    to_x.wait()
-    lower = half[column] + got_x[...]
-    out_ref[:, 0 : 2 * width] = lower
+    def columns(step):
+        return pl.ds((2 - step) * width, width)
+
+    def to_core(pair, step):
+        slot = pair * 2 + step - 1
+        return remote(
+            sums.at[1 - core, pair, :, columns(step)], got_core.at[pair, :, columns(step)],
+            red_send.at[slot], red_recv.at[slot], at(base + partners[2], side),
+        )
+
+    def to_half(pair, step):
+        slot = 4 + pair * 2 + step - 1
+        return remote(
+            sums.at[core, pair, their_rows, columns(step)], got_half.at[pair, :, columns(step)],
+            red_send.at[slot], red_recv.at[slot], at(me, 1 - side),
+        )
+
+    def to_x(pair, step):
+        slot = 8 + step - 1
+        return remote(
+            half.at[pair, :, columns(step)], got_x.at[:, columns(step)],
+            red_send.at[slot], red_recv.at[slot], at(base + partners[0], side),
+        )
+
+    steps = (2, 1)
+
+    def add_core(pair):
+        for step in steps:
+            to_core(pair, step).wait_recv()
+            sums[core, pair, their_rows, columns(step)] += got_core[pair, their_rows, columns(step)]
+            to_half(pair, step).start()
+            sums[core, pair, my_rows, columns(step)] += got_core[pair, my_rows, columns(step)]
+
+    def add_half(pair):
+        for step in steps:
+            to_half(pair, step).wait_recv()
+            half[pair, :, columns(step)] = (
+                sums[core, pair, my_rows, columns(step)] + got_half[pair, :, columns(step)]
+            )
+
+            @pl.when(column != pair)
+            def _():
+                to_x(pair, step).start()
+
+    last = chunks - 1
+
+    @pl.loop(0, last)
+    def _(chunk):
+        arrive(chunk)
+
+        @pl.when(chunk > 0)
+        def _():
+            arrive_below(chunk - 1)
+
+    arrive(last)
+    for step in steps:
+        to_core(1, step).start()
+    if last > 0:
+        arrive_below(last - 1)
+    add_core(1)
+    arrive_below(last)
+    for step in steps:
+        to_core(0, step).start()
+    add_half(1)
+    add_core(0)
+    add_half(0)
 
     def turn(step, other):
         slot = (step - 1) * 2 + other
@@ -185,14 +230,16 @@
             at(lax.rem(me + count - step, count), other),
         )
 
-    for step in (2, 1):
+    for step in steps:
+        to_x(0, step).wait_recv()
+        lower = half[column, :, columns(step)] + got_x[:, columns(step)]
         for other in (0, 1):
-            begin = (2 - step) * width + other * rows
-            turned[(step - 1) * 2 + other] = lower[:, begin : begin + rows].T
+            turned[(step - 1) * 2 + other] = lower[:, other * rows : (other + 1) * rows].T
             turn(step, other).start()
+        out_ref[:, columns(step)] = lower
     send_diag.wait()
     out_ref[:, 2 * width : 3 * width] = diag[my_rows, :] + got_diag[...]
-    for step in (2, 1):
+    for step in steps:
         for other in (0, 1):
             pltpu.make_async_copy(
                 got_turned.at[step - 1, other], got_turned.at[step - 1, other],
@@ -200,9 +247,14 @@
             ).wait()
             begin = (2 + step) * width + other * rows
             out_ref[:, begin : begin + rows] = got_turned[step - 1, other]
-    for step in (2, 1):
+    for step in steps:
         for other in (0, 1):
             turn(step, other).wait_send()
+    for step in steps:
+        to_x(0, step).wait_send()
+        for pair in (0, 1):
+            to_core(pair, step).wait_send()
+            to_half(pair, step).wait_send()
 
     @pl.loop(0, chunks)
     def _(chunk):
@@ -240,7 +292,7 @@
             pltpu.VMEM((4, rows, rows), jnp.float32),
             pltpu.VMEM((2, 2, rows, rows), jnp.float32),
             dma, dma((chunks,)), dma((3, chunks)), dma((3, chunks)),
-            dma((chunks,)), dma((chunks,)), dma((4,)), dma((4,)), dma((4,)), dma((2, 2)),
+            dma((chunks,)), dma((chunks,)), dma((11,)), dma((11,)), dma((4,)), dma((2, 2)),
         ],
         compiler_params=pltpu.CompilerParams(
             collective_id=0, has_side_effects=True, vmem_limit_bytes=48 * 1024 * 1024

time: 81.7 us -> 72 us (0.88)
  Pallas kernels: 77.5 us -> 68.3 us
    pallas_call x1, Pallas kernels: 77.5 us -> 68.3 us  [shards(): pl.pallas_call(functools.partial(kernel, count), out_shape=jax.ShapeDtype...]
where the time goes in v2:
time: 72 us; the launch traced here: 71.8 us
  Pallas kernels  68.3 us (95%)
  local copies, waits for them, and re-layouts  3.46 us (5%)
    pallas_call x1, Pallas kernels, shards(): pl.pallas_call(functools.partial(kernel, count), out_shape=jax.ShapeDtype...  68.3 us
    unnamed x3, local copies, waits for them, and re-layouts  2.7 us

profile of v2, /device:TPU:0, one launch (start us, length us, event | category | flops | bytes accessed | tf_op | source)
XLA Modules:
  0.0 71.8 jit_solution(5731155923177446593)
XLA Ops:
  0.0 0.8 %reshape.7.coulomb_ref = f32[1,6016]{1,0:T(1,128)S(1)} reshape(f32[6016]{0:T(1024)} %param.3) | data formatting | bytes 48128 | tf_op jit(solution)/shard_map/reshape | solution.py:300
  0.8 0.0 copy-start
  0.8 1.9 %copy-done = bf16[8,32,6016]{2,1,0:T(8,128)(2,1)S(1)} copy-done((bf16[8,32,6016]{2,1,0:T(8,128)(2,1)S(1)}, bf16[8,32,6016]{2,1,0:T(8,128)(2,1)}, u32[]{:S(2)}) %copy-start) | copy-done | bytes 3080216
  2.6 68.3 %shard_map.28 = f32[128,1280]{1,0:T(8,128)S(1)} custom-call(bf16[256,6016]{1,0:T(8,128)(2,1)S(1)} %bitcast.1, f32[1,6016]{1,0:T(1,128)S(1)} %reshape.7.coulomb_ref), custom_call_target="tpu_custom_call" | custom-call | tf_op jit(solution)/shard_map/pallas_call | solution.py:274
  71.0 0.8 %copy.4 = f32[128,1280]{1,0:T(8,128)} copy(f32[128,1280]{1,0:T(8,128)S(1)} %shard_map.28) | data formatting | bytes 1310720
Async XLA Ops:
  0.8 1.9 %copy-start = (bf16[8,32,6016]{2,1,0:T(8,128)(2,1)S(1)}, bf16[8,32,6016]{2,1,0:T(8,128)(2,1)}, u32[]{:S(2)}) copy-start(bf16[8,32,6016]{2,1,0:T(8,128)(2,1)} %param.2) | copy-start | bytes 9240580

commit v3 on v2

--- a/solution.py
+++ b/solution.py
@@ -24,14 +24,14 @@
 
 def plan(tiles):
     piece = -(-tiles // GROUP)
-    depth = 2 if piece % 2 == 0 else 1
+    depth = 1
     return piece, depth, piece // depth
 
 
 def kernel(
-    count, own_hbm, coulomb_ref, out_ref,
-    own_ref, slab, sums, diag, got_core, got_half, half, got_x, got_diag, turned, got_turned,
-    own_sem, local_sem, a2a_send, a2a_recv, fwd_send, fwd_recv,
+    count, own_hbm, coulomb_hbm, out_ref,
+    coulomb_ref, own_ref, slab, sums, diag, got_core, got_half, half, got_x, got_diag, turned, got_turned,
+    own_sem, coulomb_sem, local_sem, a2a_send, a2a_recv, fwd_send, fwd_recv,
     red_send, red_recv, turn_send, turn_recv,
 ):
     me = lax.axis_index("ka")
@@ -58,11 +58,7 @@
 
     barrier = pltpu.get_barrier_semaphore()
     greeted = [at(base + p, side) for p in partners]
-    greeted += [at(up, side), at(down, side), at(me, 1 - side)]
-    for shift in (1, 2):
-        for other in (0, 1):
-            greeted.append(at(lax.rem(me + shift, count), other))
-            greeted.append(at(lax.rem(me + count - shift, count), other))
+    greeted += [at(down, side), at(me, 1 - side)]
     for target in greeted:
         pl.semaphore_signal(barrier, inc=1, device_id=target, device_id_type=MESH)
 
@@ -98,6 +94,8 @@
 
     whole = pltpu.make_async_copy(own_hbm, own_ref, own_sem)
     whole.start()
+    scales = pltpu.make_async_copy(coulomb_hbm, coulomb_ref.at[0], coulomb_sem)
+    scales.start()
     for chunk in range(chunks):
         local(chunk).start()
     pl.semaphore_wait(barrier, len(greeted))
@@ -106,6 +104,7 @@
             spread(chunk, index).start()
 
     whole.wait()
+    scales.wait()
     diag[...] = jnp.zeros_like(diag)
 
     def add_diag(start, size):
@@ -121,7 +120,7 @@
     my_rows = pl.ds(pl.multiple_of(side * rows, rows), rows)
     their_rows = pl.ds(pl.multiple_of((1 - side) * rows, rows), rows)
     send_diag = remote(
-        diag.at[their_rows], got_diag, red_send.at[10], red_recv.at[10], at(me, 1 - side)
+        diag.at[their_rows], got_diag, red_send.at[20], red_recv.at[20], at(me, 1 - side)
     )
     send_diag.start()
 
@@ -155,49 +154,49 @@
         add_block(chunk, scale, 0, (2, 1))
         add_block(chunk, scale, 1, (2,))
 
-    def columns(step):
-        return pl.ds((2 - step) * width, width)
-
-    def to_core(pair, step):
-        slot = pair * 2 + step - 1
-        return remote(
-            sums.at[1 - core, pair, :, columns(step)], got_core.at[pair, :, columns(step)],
+    def columns(part):
+        return pl.ds(part * rows, rows)
+
+    def to_core(pair, part):
+        slot = pair * 4 + part
+        return remote(
+            sums.at[1 - core, pair, :, columns(part)], got_core.at[pair, :, columns(part)],
             red_send.at[slot], red_recv.at[slot], at(base + partners[2], side),
         )
 
-    def to_half(pair, step):
-        slot = 4 + pair * 2 + step - 1
-        return remote(
-            sums.at[core, pair, their_rows, columns(step)], got_half.at[pair, :, columns(step)],
+    def to_half(pair, part):
+        slot = 8 + pair * 4 + part
+        return remote(
+            sums.at[core, pair, their_rows, columns(part)], got_half.at[pair, :, columns(part)],
             red_send.at[slot], red_recv.at[slot], at(me, 1 - side),
         )
 
-    def to_x(pair, step):
-        slot = 8 + step - 1
-        return remote(
-            half.at[pair, :, columns(step)], got_x.at[:, columns(step)],
+    def to_x(pair, part):
+        slot = 16 + part
+        return remote(
+            half.at[pair, :, columns(part)], got_x.at[:, columns(part)],
             red_send.at[slot], red_recv.at[slot], at(base + partners[0], side),
         )
 
-    steps = (2, 1)
+    parts = range(4)
 
     def add_core(pair):
-        for step in steps:
-            to_core(pair, step).wait_recv()
-            sums[core, pair, their_rows, columns(step)] += got_core[pair, their_rows, columns(step)]
-            to_half(pair, step).start()
-            sums[core, pair, my_rows, columns(step)] += got_core[pair, my_rows, columns(step)]
+        for part in parts:
+            to_core(pair, part).wait_recv()
+            sums[core, pair, their_rows, columns(part)] += got_core[pair, their_rows, columns(part)]
+            to_half(pair, part).start()
+            sums[core, pair, my_rows, columns(part)] += got_core[pair, my_rows, columns(part)]
 
     def add_half(pair):
-        for step in steps:
-            to_half(pair, step).wait_recv()
-            half[pair, :, columns(step)] = (
-                sums[core, pair, my_rows, columns(step)] + got_half[pair, :, columns(step)]
+        for part in parts:
+            to_half(pair, part).wait_recv()
+            half[pair, :, columns(part)] = (
+                sums[core, pair, my_rows, columns(part)] + got_half[pair, :, columns(part)]
             )
 
             @pl.when(column != pair)
             def _():
-                to_x(pair, step).start()
+                to_x(pair, part).start()
 
     last = chunks - 1
 
@@ -210,14 +209,14 @@
             arrive_below(chunk - 1)
 
     arrive(last)
-    for step in steps:
-        to_core(1, step).start()
+    for part in parts:
+        to_core(1, part).start()
     if last > 0:
         arrive_below(last - 1)
     add_core(1)
     arrive_below(last)
-    for step in steps:
-        to_core(0, step).start()
+    for part in parts:
+        to_core(0, part).start()
     add_half(1)
     add_core(0)
     add_half(0)
@@ -230,16 +229,16 @@
             at(lax.rem(me + count - step, count), other),
         )
 
-    for step in steps:
-        to_x(0, step).wait_recv()
-        lower = half[column, :, columns(step)] + got_x[:, columns(step)]
-        for other in (0, 1):
-            turned[(step - 1) * 2 + other] = lower[:, other * rows : (other + 1) * rows].T
-            turn(step, other).start()
-        out_ref[:, columns(step)] = lower
+    for part in parts:
+        step, other = 2 - part // 2, part % 2
+        to_x(0, part).wait_recv()
+        lower = half[column, :, columns(part)] + got_x[:, columns(part)]
+        turned[(step - 1) * 2 + other] = lower.T
+        turn(step, other).start()
+        out_ref[:, columns(part)] = lower
     send_diag.wait()
     out_ref[:, 2 * width : 3 * width] = diag[my_rows, :] + got_diag[...]
-    for step in steps:
+    for step in (2, 1):
         for other in (0, 1):
             pltpu.make_async_copy(
                 got_turned.at[step - 1, other], got_turned.at[step - 1, other],
@@ -247,14 +246,14 @@
             ).wait()
             begin = (2 + step) * width + other * rows
             out_ref[:, begin : begin + rows] = got_turned[step - 1, other]
-    for step in steps:
+    for step in (2, 1):
         for other in (0, 1):
             turn(step, other).wait_send()
-    for step in steps:
-        to_x(0, step).wait_send()
+    for part in parts:
+        to_x(0, part).wait_send()
         for pair in (0, 1):
-            to_core(pair, step).wait_send()
-            to_half(pair, step).wait_send()
+            to_core(pair, part).wait_send()
+            to_half(pair, part).wait_send()
 
     @pl.loop(0, chunks)
     def _(chunk):
@@ -276,10 +275,11 @@
         out_shape=jax.ShapeDtypeStruct((rows, 5 * width), jnp.float32),
         in_specs=[
             pl.BlockSpec(memory_space=pl.ANY),
-            pl.BlockSpec(memory_space=pltpu.VMEM),
+            pl.BlockSpec(memory_space=pl.ANY),
         ],
         out_specs=pl.BlockSpec(memory_space=pltpu.VMEM),
         scratch_shapes=[
+            pltpu.VMEM((1, waves), jnp.float32),
             pltpu.VMEM((width, waves), jnp.bfloat16),
             pltpu.VMEM((chunks, GROUP + 2, width, span), jnp.bfloat16),
             pltpu.VMEM((2, 2, width, wide), jnp.float32),
@@ -291,13 +291,13 @@
             pltpu.VMEM((rows, width), jnp.float32),
             pltpu.VMEM((4, rows, rows), jnp.float32),
             pltpu.VMEM((2, 2, rows, rows), jnp.float32),
-            dma, dma((chunks,)), dma((3, chunks)), dma((3, chunks)),
-            dma((chunks,)), dma((chunks,)), dma((11,)), dma((11,)), dma((4,)), dma((2, 2)),
+            dma, dma, dma((chunks,)), dma((3, chunks)), dma((3, chunks)),
+            dma((chunks,)), dma((chunks,)), dma((21,)), dma((21,)), dma((4,)), dma((2, 2)),
         ],
         compiler_params=pltpu.CompilerParams(
-            collective_id=0, has_side_effects=True, vmem_limit_bytes=48 * 1024 * 1024
+            collective_id=0, has_side_effects=True, vmem_limit_bytes=63 * 1024 * 1024
         ),
-    )(pair_density.reshape(width, waves), coulomb.reshape(1, waves))
+    )(pair_density.reshape(width, waves), coulomb)
 
 
 def solution(mesh):

time: 72 us -> 70 us (0.972)
  local copies, waits for them, and re-layouts: 3.46 us -> 1.97 us
    reshape x1 -> x0, local copies, waits for them, and re-layouts: 0.75 us -> none  [shards(): coulomb.reshape(1, waves)]
    unnamed x3 -> x1, local copies, waits for them, and re-layouts: 2.7 us -> 1.97 us
where the time goes in v3:
time: 70 us; the launch traced here: 69.9 us
  Pallas kernels  67.9 us (97%)
  local copies, waits for them, and re-layouts  1.97 us (3%)
    pallas_call x1, Pallas kernels, shards(): pl.pallas_call(functools.partial(kernel, count), out_shape=jax.ShapeDtype...  67.9 us
    unnamed x1, local copies, waits for them, and re-layouts  1.97 us

profile of v3, /device:TPU:0, one launch (start us, length us, event | category | flops | bytes accessed | tf_op | source)
XLA Modules:
  0.0 69.9 jit_solution(8051917973278353062)
XLA Ops:
  0.0 67.9 %shard_map.28 = f32[128,1280]{1,0:T(8,128)} custom-call(bf16[256,6016]{1,0:T(8,128)(2,1)} %bitcast.1, f32[6016]{0:T(1024)} %coulomb_hbm.1), custom_call_target="tpu_custom_call" | custom-call | tf_op jit(solution)/shard_map/pallas_call | solution.py:273
  67.9 2.0 %copy.4 = f32[128,1280]{1,0:T(8,128)} copy(f32[128,1280]{1,0:T(8,128)} %shard_map.28) | data formatting | bytes 1310720
